TPU v7x, 512 devices: a whole 4x8x8 slice. The times are simulated.
512 devices in a mesh: tor: 8 (over z_lo, x), pol: 64 (over y, z_hi, core).
Axes of the slice: x: 4, y: 8, z: 8 (z_hi: 4, z_lo: 2; z = z_hi * 2 + z_lo), core: 2. Of those that a mesh axis runs over, the one named last changes fastest.
Arguments:
- plasma_state: float32 [6, 8, 512, 256], P(None, 'tor', 'pol'), may hold values from -3 to 3
- right_side: float32 [6, 8, 512, 256], P(None, 'tor', 'pol'), may hold values from -12 to 12
- resistivity: float32 [8, 512, 256], P('tor', 'pol'), may hold values from 0.05 to 0.6
- jacobi_blocks: float32 [6, 6, 8, 512, 256], P(None, None, 'tor', 'pol'), may hold values from -0.6 to 1.6, as said below
Outputs:
- update: float32 [6, 8, 512, 256], P(None, 'tor', 'pol')
- estimates: float32 [3], replicated
Inputs may be any that keep to these rules, and one draw needn't show every extreme that they name: `jacobi_blocks`: each block's diagonal entries lie in 0.4 to 1.6.
All inputs are finite; a program needn't handle non-finite values.
Results may differ from a plain program's by a relative error of at most 0.006.
Values may be sent and summed in bfloat16 or wider, within the bound.
A program may use at most 64 MiB of HBM per device.

v0:
```python
import jax
import jax.numpy as jnp
from jax import lax
from jax.sharding import PartitionSpec as P

ITERS = 3
inverse_step = 1.0
viscosity = 0.2
epsilon = 1e-06


def padded_2(cells, sides, width, closed):
    for axis, dim in sides:
        count = lax.axis_size(axis)
        ends = count if closed else count - 1
        head = lax.slice_in_dim(cells, 0, width, axis=dim)
        tail = lax.slice_in_dim(cells, cells.shape[dim] - width, cells.shape[dim], axis=dim)
        cells = jnp.concatenate(
            [
                lax.ppermute(tail, axis, [(i, (i + 1) % count) for i in range(ends)]),
                cells,
                lax.ppermute(head, axis, [((i + 1) % count, i) for i in range(ends)]),
            ],
            axis=dim,
        )
    return cells


def neighbour(values, array_axis, offset):
    length = values.shape[array_axis]
    widths = [(0, 0)] * values.ndim
    widths[array_axis] = (1, 1)
    padded = jnp.pad(values, widths)
    return lax.slice_in_dim(padded, 1 + offset, 1 + offset + length, axis=array_axis)


def linear_flux(plasma, tangent, direction):
    magnetic = plasma[0:3]
    velocity = plasma[3:6]
    tang_mag = tangent[0:3]
    tang_vel = tangent[3:6]
    pressure = jnp.sum(magnetic * tang_mag, axis=0)
    components = []
    for inner_index in range(3):
        components.append(
            tang_vel[direction] * magnetic[inner_index]
            + velocity[direction] * tang_mag[inner_index]
            - tang_mag[direction] * velocity[inner_index]
            - magnetic[direction] * tang_vel[inner_index]
        )
    for inner_index in range(3):
        moment = (
            tang_vel[direction] * velocity[inner_index]
            + velocity[direction] * tang_vel[inner_index]
            - tang_mag[direction] * magnetic[inner_index]
            - magnetic[direction] * tang_mag[inner_index]
        )
        if inner_index == direction:
            moment = moment + pressure
        components.append(moment)
    return jnp.stack(components)


def diffusion_field(resistivity):
    shape = (3,) + resistivity.shape
    return jnp.concatenate(
        [jnp.broadcast_to(resistivity[None], shape), jnp.full(shape, viscosity, jnp.float32)]
    )


def jacobian_product(
    plasma, tangent, plasma_planes, tangent_planes, plasma_rows, tangent_rows, diffusion
):
    result_sum = inverse_step * tangent
    flux_planes = linear_flux(plasma_planes, tangent_planes, 0)
    result_sum = result_sum + 0.5 * (flux_planes[:, 2:] - flux_planes[:, :-2])
    laplace_sum = tangent_planes[:, 2:] + tangent_planes[:, :-2] - 2.0 * tangent
    flux_rows = linear_flux(plasma_rows, tangent_rows, 1)
    result_sum = result_sum + 0.5 * (flux_rows[:, :, 2:] - flux_rows[:, :, :-2])
    laplace_sum = laplace_sum + tangent_rows[:, :, 2:] + tangent_rows[:, :, :-2] - 2.0 * tangent
    flux_depth = linear_flux(plasma, tangent, 2)
    result_sum = result_sum + 0.5 * (neighbour(flux_depth, 3, 1) - neighbour(flux_depth, 3, -1))
    laplace_sum = laplace_sum + neighbour(tangent, 3, 1) + neighbour(tangent, 3, -1) - 2.0 * tangent
    return result_sum - diffusion * laplace_sum


def precondition(blocks, vector):
    widened = vector.astype(jnp.float32)
    total = blocks[:, 0] * widened[0]
    for column in range(1, 6):
        total = total + blocks[:, column] * widened[column]
    return total


def least_squares(columns, initial_norm):
    count = len(columns)
    rhs_list = [initial_norm] + [jnp.float32(0.0)] * count
    cosines = []
    sines = []
    triangle = []
    estimate_list = []
    for column in range(count):
        entries = list(columns[column])
        for inner_index in range(column):
            first_value = entries[inner_index]
            second_value = entries[inner_index + 1]
            entries[inner_index] = (
                cosines[inner_index] * first_value + sines[inner_index] * second_value
            )
            entries[inner_index + 1] = (
                -sines[inner_index] * first_value + cosines[inner_index] * second_value
            )
        first_value = entries[column]
        second_value = entries[column + 1]
        radius = jnp.sqrt(first_value * first_value + second_value * second_value)
        cosine = first_value / radius
        sine_value = second_value / radius
        cosines.append(cosine)
        sines.append(sine_value)
        entries[column] = radius
        triangle.append(entries[: column + 1])
        previous = rhs_list[column]
        rhs_list[column] = cosine * previous
        rhs_list[column + 1] = -sine_value * previous
        estimate_list.append(jnp.abs(rhs_list[column + 1]))
    weights = [jnp.float32(0.0)] * count
    for column in reversed(range(count)):
        partial_value = rhs_list[column]
        for later in range(column + 1, count):
            partial_value = partial_value - triangle[later][column] * weights[later]
        weights[column] = partial_value / triangle[column][column]
    return (weights, estimate_list)


def shards(plasma_state, right_side, resistivity, jacobi_blocks):
    cell_count = (
        6
        * plasma_state.shape[1]
        * plasma_state.shape[2]
        * plasma_state.shape[3]
        * lax.axis_size("tor")
        * lax.axis_size("pol")
    )
    diffusion = diffusion_field(resistivity)
    plasma_planes = padded_2(plasma_state.astype(jnp.bfloat16), (("tor", 1),), 1, True).astype(
        plasma_state.dtype
    )
    plasma_rows = padded_2(plasma_state, (("pol", 2),), 1, False)
    square_sum = lax.psum(jnp.sum(right_side * right_side), ("tor", "pol"))
    initial_norm = jnp.sqrt(square_sum + epsilon)
    krylov_basis = [(right_side / initial_norm).astype(jnp.bfloat16)]
    directions = []
    columns = []
    for column in range(ITERS):
        vector = krylov_basis[column]
        tangent = precondition(jacobi_blocks, vector)
        tangent_planes = padded_2(tangent.astype(jnp.bfloat16), (("tor", 1),), 1, True).astype(
            tangent.dtype
        )
        tangent_rows = padded_2(tangent, (("pol", 2),), 1, False)
        image = jacobian_product(
            plasma_state,
            tangent,
            plasma_planes,
            tangent_planes,
            plasma_rows,
            tangent_rows,
            diffusion,
        )
        directions.append(tangent)
        local_products = jnp.stack(
            [jnp.sum(image * earlier.astype(jnp.float32)) for earlier in krylov_basis]
        )
        products = lax.psum(local_products, ("tor", "pol"))
        coefficients = [products[inner_index] for inner_index in range(column + 1)]
        remainder = image
        for inner_index in range(column + 1):
            remainder = remainder - coefficients[inner_index] * krylov_basis[inner_index].astype(
                jnp.float32
            )
        remainder_square = lax.psum(jnp.sum(remainder * remainder), ("tor", "pol"))
        new_norm = jnp.sqrt(remainder_square + epsilon)
        columns.append(coefficients + [new_norm])
        if column + 1 < ITERS:
            krylov_basis.append((remainder / new_norm).astype(jnp.bfloat16))
    weights, estimate_list = least_squares(columns, initial_norm)
    update = weights[0] * directions[0]
    for column in range(1, ITERS):
        update = update + weights[column] * directions[column]
    estimates = jnp.stack(estimate_list) / jnp.sqrt(jnp.float32(cell_count))
    return (update, estimates)


def solution(mesh):
    return jax.shard_map(
        shards,
        mesh=mesh,
        in_specs=(
            P(None, "tor", "pol", None),
            P(None, "tor", "pol", None),
            P("tor", "pol", None),
            P(None, None, "tor", "pol", None),
        ),
        out_specs=(P(None, "tor", "pol", None), P()),
        check_vma=False,
    )
```

profile of v0, /device:TPU:1, one launch (start us, length us, event | category | flops | bytes accessed | tf_op | source)
XLA Modules:
  0.0 785.8 jit_solution(5154822776508504955)
XLA Ops:
  0.6 1.5 multiply_reduce_fusion.5
  2.1 106.1 %psum.49 = f32[]{:T(128)} all-reduce(f32[]{:T(128)} %multiply_reduce_fusion.5), channel_id=1, replica_groups=mesh['tor'=8,'pol'=64] {'tor','pol'}, use_global_device_ids=true, to_apply=%region_1.0 | all-reduce | flops 1 | bytes 8 | tf_op jit(solution)/shard_map/psum | solution.py:149
  109.9 2.5 collective-permute-start
  112.4 4.9 collective-permute-start.1
  117.3 1.9 collective-permute-start.2
  119.3 3.0 collective-permute-start.4
  122.3 1.9 collective-permute-start.5
  124.3 4.5 collective-permute-start.6
  128.9 1.9 collective-permute-start.7
  130.9 5.8 collective-permute-start.3
  139.1 104.8 %psum.50 = f32[]{:T(128)} all-reduce(f32[]{:T(128)} %get-tuple-element.15), channel_id=1, replica_groups=mesh['tor'=8,'pol'=64] {'tor','pol'}, use_global_device_ids=true, to_apply=%region_6.7 | all-reduce | flops 1 | bytes 8 | tf_op jit(solution)/shard_map/psum | solution.py:174
  243.9 1.3 multiply_reduce_fusion.4
  245.2 95.1 %psum.51 = f32[]{:T(128)} all-reduce(f32[]{:T(128)} %multiply_reduce_fusion.4), channel_id=1, replica_groups=mesh['tor'=8,'pol'=64] {'tor','pol'}, use_global_device_ids=true, to_apply=%region_8.9 | all-reduce | flops 1 | bytes 8 | tf_op jit(solution)/shard_map/psum | solution.py:181
  341.7 3.7 collective-permute-start.8
  345.4 3.7 collective-permute-start.9
  349.2 3.1 collective-permute-start.10
  352.3 1.9 collective-permute-start.11
  356.3 1.8 collective-permute-done.11
  359.2 1.4 pad_maximum_fusion.10
  360.6 101.5 %psum.52 = f32[2]{0:T(128)S(1)} all-reduce(f32[2]{0:T(128)S(1)} %pad_maximum_fusion.10), channel_id=1, replica_groups=mesh['tor'=8,'pol'=64] {'tor','pol'}, use_global_device_ids=true, to_apply=%region_14.15 | all-reduce | flops 2 | bytes 16 | tf_op jit(solution)/shard_map/psum | solution.py:174
  462.7 1.9 multiply_reduce_fusion.2
  464.6 95.6 %psum.53 = f32[]{:T(128)} all-reduce(f32[]{:T(128)} %multiply_reduce_fusion.2), channel_id=1, replica_groups=mesh['tor'=8,'pol'=64] {'tor','pol'}, use_global_device_ids=true, to_apply=%region_16.17 | all-reduce | flops 1 | bytes 8 | tf_op jit(solution)/shard_map/psum | solution.py:181
  560.8 1.3 fusion.80
  562.2 2.8 collective-permute-start.12
  565.0 4.6 collective-permute-start.13
  569.6 3.0 collective-permute-start.14
  572.6 1.9 collective-permute-start.15
  577.4 1.1 collective-permute-done.15
  579.6 2.0 pad_maximum_fusion.11
  581.6 99.6 %psum.54 = f32[3]{0:T(128)S(1)} all-reduce(f32[3]{0:T(128)S(1)} %pad_maximum_fusion.11), channel_id=1, replica_groups=mesh['tor'=8,'pol'=64] {'tor','pol'}, use_global_device_ids=true, to_apply=%region_23.24 | all-reduce | flops 3 | bytes 24 | tf_op jit(solution)/shard_map/psum | solution.py:174
  684.4 2.6 fusion.13
  687.6 95.3 %psum.55 = f32[]{:T(128)} all-reduce(f32[]{:T(128)} %fusion.13), channel_id=1, replica_groups=mesh['tor'=8,'pol'=64] {'tor','pol'}, use_global_device_ids=true, to_apply=%region_25.26 | all-reduce | flops 1 | bytes 8 | tf_op jit(solution)/shard_map/psum | solution.py:181
  (114 shorter events, 8.7 us)
Async XLA Ops:
  0.6 108.3 %copy-start.2 = (f32[6,1,8,256]{3,2,1,0:T(8,128)S(1)}, f32[6,1,8,256]{3,2,1,0:T(8,128)}, u32[]{:S(2)}) copy-start(f32[6,1,8,256]{3,2,1,0:T(8,128)} %param.5) | copy-start | bytes 147460
  108.9 8.4 %copy-start = (f32[6,1,8,256]{3,2,1,0:T(8,128)S(1)}, f32[6,1,8,256]{3,2,1,0:T(8,128)}, u32[]{:S(2)}) copy-start(f32[6,1,8,256]{3,2,1,0:T(8,128)} %param.4) | copy-start | bytes 147460
  109.9 26.9 %collective-permute-start = (bf16[6,1,8,256]{3,2,1,0:T(8,128)(2,1)S(1)}, bf16[6,1,8,256]{3,2,1,0:T(8,128)(2,1)S(1)}, u32[]{:S(2)}, u32[]{:S(2)}) collective-permute-start(bf16[6,1,8,256]{3,2,1,0:T(8,128)(2,1)S(1)} %get-tuple-element.17), channel_id=1, source_target_pairs={{0,64},{64,128},{128,192},{192,256},{256,320},{320,384},{384,448},... | collective-permute-start | bytes 73736 | tf_op jit(solution)/shard_map/ppermute | solution.py:20
  112.4 24.4 %collective-permute-start.1 = (bf16[6,1,8,256]{3,2,1,0:T(8,128)(2,1)S(1)}, bf16[6,1,8,256]{3,2,1,0:T(8,128)(2,1)S(1)}, u32[]{:S(2)}, u32[]{:S(2)}) collective-permute-start(bf16[6,1,8,256]{3,2,1,0:T(8,128)(2,1)S(1)} %get-tuple-element.17), channel_id=1, source_target_pairs={{64,0},{128,64},{192,128},{256,192},{320,256},{384,320},{448,384},... | collective-permute-start | bytes 73736 | tf_op jit(solution)/shard_map/ppermute | solution.py:22
  117.3 19.5 %collective-permute-start.2 = (bf16[6,1,8,256]{3,2,1,0:T(8,128)(2,1)S(1)}, bf16[6,1,8,256]{3,2,1,0:T(8,128)(2,1)S(1)}, u32[]{:S(2)}, u32[]{:S(2)}) collective-permute-start(bf16[6,1,8,256]{3,2,1,0:T(8,128)(2,1)S(1)} %convert_element_type.95), channel_id=1, source_target_pairs={{0,64},{64,128},{128,192},{192,256},{256,320},{320,384},{384,448},... | collective-permute-start | bytes 73736 | tf_op jit(solution)/shard_map/ppermute | solution.py:20
  119.3 5.1 collective-permute-start.4
  122.3 6.6 collective-permute-start.5
  124.3 6.5 collective-permute-start.6
  128.9 7.7 collective-permute-start.7
  130.9 6.7 collective-permute-start.3
  137.7 0.7 copy-start.3
  139.1 202.6 %copy-start.1 = (f32[6,6,1,8,256]{4,3,2,1,0:T(8,128)S(1)}, f32[6,6,1,8,256]{4,3,2,1,0:T(8,128)}, u32[]{:S(2)}) copy-start(f32[6,6,1,8,256]{4,3,2,1,0:T(8,128)} %param.7) | copy-start | bytes 884740
  341.7 16.6 %collective-permute-start.8 = (bf16[6,1,8,256]{3,2,1,0:T(8,128)(2,1)S(1)}, bf16[6,1,8,256]{3,2,1,0:T(8,128)(2,1)S(1)}, u32[]{:S(2)}, u32[]{:S(2)}) collective-permute-start(bf16[6,1,8,256]{3,2,1,0:T(8,128)(2,1)S(1)} %get-tuple-element.11), channel_id=1, source_target_pairs={{0,64},{64,128},{128,192},{192,256},{256,320},{320,384},{384,448},... | collective-permute-start | bytes 73736 | tf_op jit(solution)/shard_map/ppermute | solution.py:20
  345.4 12.9 %collective-permute-start.9 = (bf16[6,1,8,256]{3,2,1,0:T(8,128)(2,1)S(1)}, bf16[6,1,8,256]{3,2,1,0:T(8,128)(2,1)S(1)}, u32[]{:S(2)}, u32[]{:S(2)}) collective-permute-start(bf16[6,1,8,256]{3,2,1,0:T(8,128)(2,1)S(1)} %get-tuple-element.11), channel_id=1, source_target_pairs={{64,0},{128,64},{192,128},{256,192},{320,256},{384,320},{448,384},... | collective-permute-start | bytes 73736 | tf_op jit(solution)/shard_map/ppermute | solution.py:22
  349.2 7.2 collective-permute-start.10
  352.3 5.8 collective-permute-start.11
  562.2 16.5 %collective-permute-start.12 = (bf16[6,1,8,256]{3,2,1,0:T(8,128)(2,1)S(1)}, bf16[6,1,8,256]{3,2,1,0:T(8,128)(2,1)S(1)}, u32[]{:S(2)}, u32[]{:S(2)}) collective-permute-start(bf16[6,1,8,256]{3,2,1,0:T(8,128)(2,1)S(1)} %get-tuple-element.8), channel_id=1, source_target_pairs={{0,64},{64,128},{128,192},{192,256},{256,320},{320,384},{384,448},... | collective-permute-start | bytes 73736 | tf_op jit(solution)/shard_map/ppermute | solution.py:20
  565.0 13.7 %collective-permute-start.13 = (bf16[6,1,8,256]{3,2,1,0:T(8,128)(2,1)S(1)}, bf16[6,1,8,256]{3,2,1,0:T(8,128)(2,1)S(1)}, u32[]{:S(2)}, u32[]{:S(2)}) collective-permute-start(bf16[6,1,8,256]{3,2,1,0:T(8,128)(2,1)S(1)} %get-tuple-element.8), channel_id=1, source_target_pairs={{64,0},{128,64},{192,128},{256,192},{320,256},{384,320},{448,384},... | collective-permute-start | bytes 73736 | tf_op jit(solution)/shard_map/ppermute | solution.py:22
  569.6 7.7 collective-permute-start.14
  572.6 5.8 collective-permute-start.15
where the time goes:
time: 787 us; the launch traced here: 786 us
  blocking collectives  698 us (89%)
  starting transfers between devices  51.1 us (6%)
  other arithmetic  18 us (2%)
  between operations  13.1 us (2%)
    psum x3, blocking collectives, shards(): products = lax.psum(local_products, ('tor', 'pol'))  306 us
    psum x3, blocking collectives, shards(): remainder_square = lax.psum(jnp.sum(remainder * remainder), ('tor', 'pol'))  286 us
    psum x1, blocking collectives, shards(): square_sum = lax.psum(jnp.sum(right_side * right_side), ('tor', 'pol'))  106 us
    ppermute x8, starting transfers between devices, padded_2(): lax.ppermute(head, axis, [((i + 1) % count, i) for i in range(ends)])  26.7 us
    ppermute x8, starting transfers between devices, padded_2(): lax.ppermute(tail, axis, [(i, (i + 1) % count) for i in range(ends)])  24.5 us
  transfers between devices with their start and end apart: 16, of which 3 were waited for; matrix products, arithmetic and copies ran while one was open for 0% of the time, Pallas kernels for 0%

commit v1 on v0

--- a/solution.py
+++ b/solution.py
@@ -171,7 +171,7 @@
         local_products = jnp.stack(
             [jnp.sum(image * earlier.astype(jnp.float32)) for earlier in krylov_basis]
         )
-        products = lax.psum(local_products, ("tor", "pol"))
+        products = lax.psum(lax.psum(local_products, "pol"), "tor")
         coefficients = [products[inner_index] for inner_index in range(column + 1)]
         remainder = image
         for inner_index in range(column + 1):

time: 787 us -> 973 us (1.24)
  blocking collectives: 698 us -> 881 us
    psum x3 -> x6, blocking collectives: 306 us -> 452 us  [shards(): products = lax.psum(lax.psum(local_products, 'pol'), 'tor')]
    psum x3, blocking collectives: 286 us -> 323 us  [shards(): remainder_square = lax.psum(jnp.sum(remainder * remainder), ('tor', 'pol'))]
where the time goes in v1:
time: 973 us; the launch traced here: 971 us
  blocking collectives  881 us (91%)
  starting transfers between devices  53.3 us (5%)
  other arithmetic  18 us (2%)
  between operations  13.1 us (1%)
    psum x6, blocking collectives, shards(): products = lax.psum(lax.psum(local_products, 'pol'), 'tor')  452 us
    psum x3, blocking collectives, shards(): remainder_square = lax.psum(jnp.sum(remainder * remainder), ('tor', 'pol'))  323 us
    psum x1, blocking collectives, shards(): square_sum = lax.psum(jnp.sum(right_side * right_side), ('tor', 'pol'))  106 us
    ppermute x8, starting transfers between devices, padded_2(): lax.ppermute(tail, axis, [(i, (i + 1) % count) for i in range(ends)])  27.3 us
    ppermute x8, starting transfers between devices, padded_2(): lax.ppermute(head, axis, [((i + 1) % count, i) for i in range(ends)])  26 us
  transfers between devices with their start and end apart: 16, of which 3 were waited for; matrix products, arithmetic and copies ran while one was open for 0% of the time, Pallas kernels for 0%

profile of v1, /device:TPU:1, one launch (start us, length us, event | category | flops | bytes accessed | tf_op | source)
XLA Modules:
  0.0 971.2 jit_solution(2014521607667818468)
XLA Ops:
  0.6 1.5 multiply_reduce_fusion.5
  2.1 106.1 %psum.70 = f32[]{:T(128)} all-reduce(f32[]{:T(128)} %multiply_reduce_fusion.5), channel_id=1, replica_groups=mesh['tor'=8,'pol'=64] {'tor','pol'}, use_global_device_ids=true, to_apply=%region_1.0 | all-reduce | flops 1 | bytes 8 | tf_op jit(solution)/shard_map/psum | solution.py:149
  109.9 2.5 collective-permute-start
  112.4 4.9 collective-permute-start.1
  117.3 1.9 collective-permute-start.2
  119.3 3.0 collective-permute-start.4
  122.3 1.9 collective-permute-start.5
  124.3 4.5 collective-permute-start.6
  128.9 1.9 collective-permute-start.7
  130.9 5.8 collective-permute-start.3
  139.1 138.6 %psum.71 = f32[1]{0:T(128)} all-reduce(f32[1]{0:T(128)} %bitcast.16), channel_id=1, replica_groups=mesh['tor'=8,'pol'=64] {'pol'}, use_global_device_ids=true, to_apply=%region_6.7 | all-reduce | flops 1 | bytes 8 | tf_op jit(solution)/shard_map/psum | solution.py:174
  277.8 17.2 %psum.72 = f32[]{:T(128)} all-reduce(f32[]{:T(128)} %bitcast.17), channel_id=1, replica_groups=mesh['tor'=8,'pol'=64] {'tor'}, use_global_device_ids=true, to_apply=%region_7.8 | all-reduce | flops 1 | bytes 8 | tf_op jit(solution)/shard_map/psum | solution.py:174
  296.2 106.4 %psum.73 = f32[]{:T(128)} all-reduce(f32[]{:T(128)} %multiply_reduce_fusion.4), channel_id=1, replica_groups=mesh['tor'=8,'pol'=64] {'tor','pol'}, use_global_device_ids=true, to_apply=%region_9.10 | all-reduce | flops 1 | bytes 8 | tf_op jit(solution)/shard_map/psum | solution.py:181
  404.1 3.7 collective-permute-start.8
  407.8 3.7 collective-permute-start.9
  411.6 4.1 collective-permute-start.10
  415.7 1.9 collective-permute-start.11
  419.7 1.8 collective-permute-done.11
  422.6 1.4 pad_maximum_fusion.10
  424.0 135.0 %psum.74 = f32[2]{0:T(128)S(1)} all-reduce(f32[2]{0:T(128)S(1)} %pad_maximum_fusion.10), channel_id=1, replica_groups=mesh['tor'=8,'pol'=64] {'pol'}, use_global_device_ids=true, to_apply=%region_15.16 | all-reduce | flops 2 | bytes 16 | tf_op jit(solution)/shard_map/psum | solution.py:174
  559.0 12.5 %psum.75 = f32[2]{0:T(128)S(1)} all-reduce(f32[2]{0:T(128)S(1)} %psum.74), channel_id=1, replica_groups=mesh['tor'=8,'pol'=64] {'tor'}, use_global_device_ids=true, to_apply=%region_16.17 | all-reduce | flops 2 | bytes 16 | tf_op jit(solution)/shard_map/psum | solution.py:174
  572.1 1.9 multiply_reduce_fusion.2
  574.0 108.6 %psum.76 = f32[]{:T(128)} all-reduce(f32[]{:T(128)} %multiply_reduce_fusion.2), channel_id=1, replica_groups=mesh['tor'=8,'pol'=64] {'tor','pol'}, use_global_device_ids=true, to_apply=%region_18.19 | all-reduce | flops 1 | bytes 8 | tf_op jit(solution)/shard_map/psum | solution.py:181
  684.5 3.5 collective-permute-start.12
  688.0 3.9 collective-permute-start.13
  692.0 4.1 collective-permute-start.14
  696.1 1.9 collective-permute-start.15
  703.1 2.0 pad_maximum_fusion.11
  705.1 136.2 %psum.77 = f32[3]{0:T(128)S(1)} all-reduce(f32[3]{0:T(128)S(1)} %pad_maximum_fusion.11), channel_id=1, replica_groups=mesh['tor'=8,'pol'=64] {'pol'}, use_global_device_ids=true, to_apply=%region_25.26 | all-reduce | flops 3 | bytes 24 | tf_op jit(solution)/shard_map/psum | solution.py:174
  841.3 12.5 %psum.78 = f32[3]{0:T(128)S(1)} all-reduce(f32[3]{0:T(128)S(1)} %psum.77), channel_id=1, replica_groups=mesh['tor'=8,'pol'=64] {'tor'}, use_global_device_ids=true, to_apply=%region_26.27 | all-reduce | flops 3 | bytes 24 | tf_op jit(solution)/shard_map/psum | solution.py:174
  856.9 2.6 fusion.13
  860.2 108.1 %psum.79 = f32[]{:T(128)} all-reduce(f32[]{:T(128)} %fusion.13), channel_id=1, replica_groups=mesh['tor'=8,'pol'=64] {'tor','pol'}, use_global_device_ids=true, to_apply=%region_28.29 | all-reduce | flops 1 | bytes 8 | tf_op jit(solution)/shard_map/psum | solution.py:181
  (117 shorter events, 12.4 us)
Async XLA Ops:
  0.6 108.3 %copy-start.2 = (f32[6,1,8,256]{3,2,1,0:T(8,128)S(1)}, f32[6,1,8,256]{3,2,1,0:T(8,128)}, u32[]{:S(2)}) copy-start(f32[6,1,8,256]{3,2,1,0:T(8,128)} %param.5) | copy-start | bytes 147460
  108.9 8.4 copy-start
  109.9 26.9 %collective-permute-start = (bf16[6,1,8,256]{3,2,1,0:T(8,128)(2,1)S(1)}, bf16[6,1,8,256]{3,2,1,0:T(8,128)(2,1)S(1)}, u32[]{:S(2)}, u32[]{:S(2)}) collective-permute-start(bf16[6,1,8,256]{3,2,1,0:T(8,128)(2,1)S(1)} %get-tuple-element.17), channel_id=1, source_target_pairs={{0,64},{64,128},{128,192},{192,256},{256,320},{320,384},{384,448},... | collective-permute-start | bytes 73736 | tf_op jit(solution)/shard_map/ppermute | solution.py:20
  112.4 24.4 %collective-permute-start.1 = (bf16[6,1,8,256]{3,2,1,0:T(8,128)(2,1)S(1)}, bf16[6,1,8,256]{3,2,1,0:T(8,128)(2,1)S(1)}, u32[]{:S(2)}, u32[]{:S(2)}) collective-permute-start(bf16[6,1,8,256]{3,2,1,0:T(8,128)(2,1)S(1)} %get-tuple-element.17), channel_id=1, source_target_pairs={{64,0},{128,64},{192,128},{256,192},{320,256},{384,320},{448,384},... | collective-permute-start | bytes 73736 | tf_op jit(solution)/shard_map/ppermute | solution.py:22
  117.3 19.5 %collective-permute-start.2 = (bf16[6,1,8,256]{3,2,1,0:T(8,128)(2,1)S(1)}, bf16[6,1,8,256]{3,2,1,0:T(8,128)(2,1)S(1)}, u32[]{:S(2)}, u32[]{:S(2)}) collective-permute-start(bf16[6,1,8,256]{3,2,1,0:T(8,128)(2,1)S(1)} %convert_element_type.95), channel_id=1, source_target_pairs={{0,64},{64,128},{128,192},{192,256},{256,320},{320,384},{384,448},... | collective-permute-start | bytes 73736 | tf_op jit(solution)/shard_map/ppermute | solution.py:20
  119.3 5.1 collective-permute-start.4
  122.3 6.6 collective-permute-start.5
  124.3 6.5 collective-permute-start.6
  128.9 7.7 collective-permute-start.7
  130.9 6.7 collective-permute-start.3
  137.7 0.7 copy-start.3
  139.1 264.9 %copy-start.1 = (f32[6,6,1,8,256]{4,3,2,1,0:T(8,128)S(1)}, f32[6,6,1,8,256]{4,3,2,1,0:T(8,128)}, u32[]{:S(2)}) copy-start(f32[6,6,1,8,256]{4,3,2,1,0:T(8,128)} %param.7) | copy-start | bytes 884740
  404.1 17.6 %collective-permute-start.8 = (bf16[6,1,8,256]{3,2,1,0:T(8,128)(2,1)S(1)}, bf16[6,1,8,256]{3,2,1,0:T(8,128)(2,1)S(1)}, u32[]{:S(2)}, u32[]{:S(2)}) collective-permute-start(bf16[6,1,8,256]{3,2,1,0:T(8,128)(2,1)S(1)} %get-tuple-element.11), channel_id=1, source_target_pairs={{0,64},{64,128},{128,192},{192,256},{256,320},{320,384},{384,448},... | collective-permute-start | bytes 73736 | tf_op jit(solution)/shard_map/ppermute | solution.py:20
  407.8 13.9 %collective-permute-start.9 = (bf16[6,1,8,256]{3,2,1,0:T(8,128)(2,1)S(1)}, bf16[6,1,8,256]{3,2,1,0:T(8,128)(2,1)S(1)}, u32[]{:S(2)}, u32[]{:S(2)}) collective-permute-start(bf16[6,1,8,256]{3,2,1,0:T(8,128)(2,1)S(1)} %get-tuple-element.11), channel_id=1, source_target_pairs={{64,0},{128,64},{192,128},{256,192},{320,256},{384,320},{448,384},... | collective-permute-start | bytes 73736 | tf_op jit(solution)/shard_map/ppermute | solution.py:22
  411.6 8.2 collective-permute-start.10
  415.7 5.8 collective-permute-start.11
  684.5 17.6 %collective-permute-start.12 = (bf16[6,1,8,256]{3,2,1,0:T(8,128)(2,1)S(1)}, bf16[6,1,8,256]{3,2,1,0:T(8,128)(2,1)S(1)}, u32[]{:S(2)}, u32[]{:S(2)}) collective-permute-start(bf16[6,1,8,256]{3,2,1,0:T(8,128)(2,1)S(1)} %get-tuple-element.8), channel_id=1, source_target_pairs={{0,64},{64,128},{128,192},{192,256},{256,320},{320,384},{384,448},... | collective-permute-start | bytes 73736 | tf_op jit(solution)/shard_map/ppermute | solution.py:20
  688.0 14.1 %collective-permute-start.13 = (bf16[6,1,8,256]{3,2,1,0:T(8,128)(2,1)S(1)}, bf16[6,1,8,256]{3,2,1,0:T(8,128)(2,1)S(1)}, u32[]{:S(2)}, u32[]{:S(2)}) collective-permute-start(bf16[6,1,8,256]{3,2,1,0:T(8,128)(2,1)S(1)} %get-tuple-element.8), channel_id=1, source_target_pairs={{64,0},{128,64},{192,128},{256,192},{320,256},{384,320},{448,384},... | collective-permute-start | bytes 73736 | tf_op jit(solution)/shard_map/ppermute | solution.py:22
  692.0 8.9 collective-permute-start.14
  696.1 5.8 collective-permute-start.15
